TPU v7x, 32 devices: a whole 2x2x4 slice. The times are simulated.
32 devices in a mesh: dp: 8 (over z, x), mp: 4 (over y, core).
Axes of the slice: x: 2, y: 2, z: 4, core: 2. Of those that a mesh axis runs over, the one named last changes fastest.
Arguments:
- activations: bfloat16 [4096, 2560], P('dp'), may hold values from -6 to 6
- cotangent: bfloat16 [4096, 6912], P('dp', 'mp'), may hold values from -6 to 6
- frozen_weight: bfloat16 [2560, 6912], P(None, 'mp'), may hold values from -0.078125 to 0.078125
- skew_params: bfloat16 [10, 256, 256], replicated, may hold values from -0.125 to 0.125
- tile_order: int32 [20], replicated, may hold values from 0 to 19, each once
- block_owner: int32 [10], replicated, may hold values from 0 to 7, as said below
Outputs:
- input_grad: bfloat16 [4096, 2560], P('dp', 'mp')
- skew_grads: float32 [24, 256, 256], P('dp')
Inputs may be any that keep to these rules, and one draw needn't show every extreme that they name: `tile_order`: a permutation of the 20 tiles. `block_owner`: no index of dp owns more than 3 blocks, and some index owns exactly 3; indices 0 and 8 - 1 own blocks in every draw.
All inputs are finite; a program needn't handle non-finite values.
Results may differ from a plain program's by a relative error of at most 0.001.
Values sent between devices are 32-bit elements; how exact they have to be, the bound alone decides.
A program may use at most 128 MiB of HBM per device.

v0:
```python
import functools
import math

import jax
import jax.numpy as jnp
from jax import lax
from jax.experimental import pallas as pl
from jax.experimental.pallas import tpu as pltpu
from jax.sharding import PartitionSpec as P

SLOTS = 3
LANES = 128
CHUNKS = 2
MESH = pl.DeviceIdType.MESH
F32 = jnp.float32
BF16 = jnp.bfloat16

NN = (((1,), (0,)), ((), ()))
NT = (((1,), (1,)), ((), ()))
TN = (((0,), (0,)), ((), ()))


def dot(a, b, dims=NN):
    return lax.dot_general(a, b, dims, preferred_element_type=F32)


def split(x):
    high = x.astype(BF16)
    return high, (x - high.astype(F32)).astype(BF16)


def dot_split(a, b):
    return dot(a[0], b[0]) + (dot(a[0], b[1]) + dot(a[1], b[0]))


def skew_of(params):
    plain = params.astype(F32)
    return plain - plain.T


def kernel(cfg, order_ref, owner_ref, act_hbm, cot_hbm, w_hbm, s_hbm, out_ref, grad_ref, *scratch):
    tokens, dim, block, blocks, tiles, n_dp, n_mp, own_gram = cfg
    (inv_ref, idx_ref, valid_ref, act_ref, cot_ref, cots, w_ref, s_ref, ls, acts, feat, outblk, part, eth, etl, recv1, send2, recv2, gram, grecv, gsum, arecv, hsum, zrecv, gpart, yrecv, gfull,
     slot_out, slot_in, slot_mate, s1, r1, s2, r2, gs, gr, xs, xr, ds, dr, ys, yr, ss, sr, ms, mr) = scratch
    half_mp = n_mp // 2
    rows = tokens // CHUNKS
    per = tiles // n_mp
    piece = block // 2 // n_dp
    dp = lax.axis_index("dp")
    mp = lax.axis_index("mp")
    side = lax.rem(mp, 2)
    group = mp // 2
    mate = group * 2 + (1 - side)

    load_s = pltpu.make_async_copy(s_hbm, s_ref, ls.at[blocks])
    load_cot = pltpu.make_async_copy(cot_hbm, cot_ref, ls.at[blocks + 1])
    load_act = pltpu.make_async_copy(act_hbm, act_ref, ls.at[blocks + 2])

    def load_w(n):
        at = pl.ds(pl.multiple_of(n * block, block), block)
        return pltpu.make_async_copy(w_hbm.at[:, at], w_ref.at[:, at], ls.at[n])

    load_s.start()
    load_cot.start()
    for n in range(blocks):
        load_w(n).start()
    load_act.start()

    def same_side(offset):
        return lax.rem(group + offset, half_mp)

    barrier = pltpu.get_barrier_semaphore()
    peers = []
    for o in range(half_mp):
        for k in range(2):
            if o or k:
                q = same_side(o)
                peers.append((dp, q * 2 + (side if k == 0 else 1 - side)))
    if own_gram:
        for o in range(1, n_dp):
            peers.append((lax.rem(dp + o, n_dp), mp))
    for peer in peers:
        pl.semaphore_signal(barrier, inc=1, device_id=peer, device_id_type=MESH)

    def invert(k, _):
        found = jnp.int32(0)
        for i in range(tiles):
            found = jnp.where(order_ref[i] == k, i, found)
        inv_ref[k] = found
        return 0

    lax.fori_loop(0, tiles, invert, 0)
    if own_gram:
        places = []
        for b in range(blocks):
            place = owner_ref[b] * SLOTS
            for e in range(b):
                place = place + jnp.where(owner_ref[e] == owner_ref[b], 1, 0)
            places.append(place)

        def locate(q, _):
            found = jnp.int32(0)
            count = jnp.float32(0.0)
            for b in range(blocks):
                found = jnp.where(places[b] == q, b, found)
                count = jnp.where(places[b] == q, 1.0, count)
            idx_ref[q] = found
            valid_ref[q] = count
            return 0

        lax.fori_loop(0, n_dp * SLOTS, locate, 0)

    def rotation(b, _):
        skew = skew_of(s_ref[b])
        pair = split(skew)
        square = dot_split(pair, pair)
        cube = dot_split(split(square), pair)
        high, low = split(2.0 * square - 2.0 * skew - cube)
        eth[b] = high
        etl[b] = low
        return 0

    load_s.wait()
    lax.fori_loop(0, blocks, rotation, 0)
    load_cot.wait()
    for i in range(tokens // LANES):
        cots[i * LANES:(i + 1) * LANES, :] = cot_ref[:, i * LANES:(i + 1) * LANES].T

    def features(j):
        def body(n, _):
            if j == 0:
                load_w(n).wait()
            f = dot(cots[j * rows:(j + 1) * rows, :], w_ref[:, pl.ds(pl.multiple_of(n * block, block), block)])
            feat[j * tiles + 2 * n] = f[:, :LANES]
            feat[j * tiles + 2 * n + 1] = f[:, LANES:]
            return 0
        lax.fori_loop(0, blocks, body, 0)

    def rotate(j):
        def body(b, _):
            t0 = order_ref[2 * b]
            t1 = order_ref[2 * b + 1]
            f = jnp.concatenate([feat[j * tiles + t0], feat[j * tiles + t1]], axis=1)
            high, low = split(f)
            out = f + (dot(high, eth[b]) + (dot(low, eth[b]) + dot(high, etl[b])))
            outblk[2 * b] = out[:, :LANES]
            outblk[2 * b + 1] = out[:, LANES:]
            return 0
        lax.fori_loop(0, blocks, body, 0)

    def grams():
        load_act.wait()
        for j in range(CHUNKS):
            for k in range(tiles):
                acts[j * tiles + k] = act_ref[j * rows:(j + 1) * rows, k * LANES:(k + 1) * LANES]

        def body(b, _):
            t0 = order_ref[2 * b]
            t1 = order_ref[2 * b + 1]
            g = 0.0
            for j in range(CHUNKS):
                f = jnp.concatenate([feat[j * tiles + t0], feat[j * tiles + t1]], axis=1)
                x = jnp.concatenate([acts[j * tiles + t0], acts[j * tiles + t1]], axis=1)
                high, low = split(f)
                g = g + (dot(x, high, TN) + dot(x, low, TN))
            if own_gram:
                for h in range(2):
                    for p in range(n_dp):
                        at = (h * n_dp + p) * piece
                        gram[h, p, b] = g[at:at + piece]
            else:
                grad_ref[b] = g
            return 0
        lax.fori_loop(0, blocks, body, 0)

    def permute(j):
        for q in range(n_mp):
            def body(i, _):
                part[j, q, i] = outblk[inv_ref[q * per + i]]
                return 0
            lax.fori_loop(0, per, body, 0)

    def first(j, o):
        q = same_side(o)
        return pltpu.make_async_remote_copy(
            src_ref=part.at[j, q * 2 + (1 - side)], dst_ref=recv1.at[j, q],
            send_sem=s1.at[j, o], recv_sem=r1.at[j, o],
            device_id=(dp, mate), device_id_type=MESH)

    def second(j, o):
        q = same_side(o)
        return pltpu.make_async_remote_copy(
            src_ref=send2.at[j, o - 1], dst_ref=recv2.at[j, o - 1],
            send_sem=s2.at[j, o - 1], recv_sem=r2.at[j, o - 1],
            device_id=(dp, q * 2 + side), device_id_type=MESH)

    order1 = list(range(1, half_mp)) + [0]

    def start_first(j):
        for o in order1:
            first(j, o).start()

    def start_second(j):
        for o in range(1, half_mp):
            first(j, o).wait_recv()
            q = same_side(o)
            for i in range(per):
                send2[j, o - 1, i] = part[j, q * 2 + side, i] + recv1[j, q, i]
            second(j, o).start()

    def finish(j):
        first(j, 0).wait_recv()
        for o in range(1, half_mp):
            second(j, o).wait_recv()
        for i in range(per):
            total = part[j, mp, i] + recv1[j, group, i]
            for o in range(1, half_mp):
                total = total + recv2[j, o - 1, i]
            out_ref[j * rows:(j + 1) * rows, i * LANES:(i + 1) * LANES] = total.astype(out_ref.dtype)

    features(0)
    rotate(0)
    permute(0)
    pl.semaphore_wait(barrier, len(peers))
    start_first(0)
    for j in range(1, CHUNKS):
        features(j)
        start_second(j - 1)
        if j == CHUNKS - 1:
            grams()
            if own_gram:
                swap = pltpu.make_async_remote_copy(
                    src_ref=gram.at[1 - side], dst_ref=grecv, send_sem=gs.at[0], recv_sem=gr.at[0],
                    device_id=(dp, mate), device_id_type=MESH)
                swap.start()
        rotate(j)
        permute(j)
        start_first(j)
    last = CHUNKS - 1

    start_second(last)
    if own_gram:
        swap.wait_recv()

        parity = lax.rem(dp, 2)
        line = dp // 2
        n_line = n_dp // 2
        parts = gsum.shape[1]
        some = blocks // parts

        def cross(g):
            return pltpu.make_async_remote_copy(
                src_ref=gsum.at[1 - parity, g], dst_ref=arecv.at[g], send_sem=xs.at[g], recv_sem=xr.at[g],
                device_id=(dp + 1 - 2 * parity, mp), device_id_type=MESH)

        def along(g, o):
            to = lax.rem(line + o, n_line)
            return pltpu.make_async_remote_copy(
                src_ref=hsum.at[g, to], dst_ref=zrecv.at[g, o - 1],
                send_sem=ds.at[g, o - 1], recv_sem=dr.at[g, o - 1],
                device_id=(to * 2 + parity, mp), device_id_type=MESH)

        for g in range(parts):
            def add_half(q, _):
                own = pl.ds(g * some, some)
                for t in range(2):
                    gsum[t, g, q] = gram[side, 2 * q + t, own] + grecv[2 * q + t, own]
                return 0
            lax.fori_loop(0, n_line, add_half, 0)
            cross(g).start()
        for g in range(parts):
            cross(g).wait_recv()

            def add_cross(q, _):
                hsum[g, q] = gsum[parity, g, q] + arecv[g, q]
                return 0
            lax.fori_loop(0, n_line, add_cross, 0)
            for o in range(1, n_line):
                along(g, o).start()
        for j in range(last):
            finish(j)

        def turn(s, _):
            eth[s], etl[s] = split(-skew_of(s_ref[idx_ref[dp * SLOTS + s]]))
            return 0
        lax.fori_loop(0, SLOTS, turn, 0)
        for g in range(parts):
            for o in range(1, n_line):
                along(g, o).wait_recv()
            total = hsum[g, line]
            for o in range(1, n_line):
                total = total + zrecv[g, o - 1]
            gpart[g * some:(g + 1) * some] = total

        def across(o):
            return pltpu.make_async_remote_copy(
                src_ref=gpart, dst_ref=yrecv.at[o - 1],
                send_sem=ys.at[o - 1], recv_sem=yr.at[o - 1],
                device_id=(dp, same_side(o) * 2 + side), device_id_type=MESH)

        for o in range(1, half_mp):
            across(o).start()
        for o in range(1, half_mp):
            across(o).wait_recv()

        def add_y(b, _):
            total = gpart[b]
            for o in range(1, half_mp):
                total = total + yrecv[o - 1, b]
            gfull[b] = total
            return 0
        lax.fori_loop(0, blocks, add_y, 0)

        for d in range(n_dp):
            for s in range(SLOTS):
                slot_out[d, s] = gfull[idx_ref[d * SLOTS + s]] * valid_ref[d * SLOTS + s]

        def deliver(o):
            to = lax.rem(dp + o, n_dp)
            return pltpu.make_async_remote_copy(
                src_ref=slot_out.at[to], dst_ref=slot_in.at[dp],
                send_sem=ss.at[o], recv_sem=sr.at[o],
                device_id=(to, mp), device_id_type=MESH)

        for o in range(1, n_dp):
            deliver(o).start()
        mine = pltpu.make_async_copy(slot_out.at[dp], slot_in.at[dp], ss.at[0])
        mine.start()
        mine.wait()
        finish(last)
        for o in range(1, n_dp):
            deliver(o).wait_recv()
        share = pltpu.make_async_remote_copy(
            src_ref=slot_in, dst_ref=slot_mate, send_sem=ms.at[0], recv_sem=mr.at[0],
            device_id=(dp, mate), device_id_type=MESH)
        share.start()
        share.wait_recv()
        upper = jnp.where(side == 0, 0.0, 1.0)

        def adjoint(s, _):
            own = jnp.concatenate([slot_in[p, s] for p in range(n_dp)], axis=0)
            other = jnp.concatenate([slot_mate[p, s] for p in range(n_dp)], axis=0)
            g = jnp.concatenate([own * (1.0 - upper) + other * upper, own * upper + other * (1.0 - upper)], axis=0)
            qt = (eth[s], etl[s])
            gp = split(g)
            left = dot_split(gp, qt)
            both = left + dot_split(qt, gp)
            total = 2.0 * g + 2.0 * both + dot_split(split(left), qt) + dot_split(qt, split(both))
            grad_ref[s] = (total - total.T) * (1.0 / math.sqrt(tokens * n_dp))
            return 0
        lax.fori_loop(0, SLOTS, adjoint, 0)
        swap.wait_send()
        for g in range(parts):
            cross(g).wait_send()
            for o in range(1, n_line):
                along(g, o).wait_send()
        for o in range(1, half_mp):
            across(o).wait_send()
        share.wait_send()
        for o in range(1, n_dp):
            deliver(o).wait_send()
    else:
        for j in range(CHUNKS):
            finish(j)
    for j in range(CHUNKS):
        for o in range(half_mp):
            first(j, o).wait_send()
        for o in range(1, half_mp):
            second(j, o).wait_send()


def local(n_dp, n_mp, activations, cotangent, frozen_weight, skew_params, tile_order, block_owner):
    tokens, dim = activations.shape
    hidden = cotangent.shape[1]
    blocks, block, _ = skew_params.shape
    tiles = tile_order.shape[0]
    piece = block // 2 // n_dp
    own_gram = piece * n_dp * 2 == block and piece % 8 == 0 and n_dp % 2 == 0
    keep = piece if own_gram else 8
    ring = n_dp if own_gram else 2
    width = blocks if own_gram else 1
    parts = next(k for k in (5, 2, 1) if width % k == 0)
    half_mp = n_mp // 2
    rows = tokens // CHUNKS
    per = tiles // n_mp

    cfg = (tokens, dim, block, blocks, tiles, n_dp, n_mp, own_gram)
    smem = pl.BlockSpec(memory_space=pltpu.SMEM)
    vmem = pl.BlockSpec(memory_space=pltpu.VMEM)
    dma = pltpu.SemaphoreType.DMA
    span = max(half_mp - 1, 1)
    grad_shape = (SLOTS if own_gram else blocks, block, block)
    input_grad, grads = pl.pallas_call(
        functools.partial(kernel, cfg),
        out_shape=(jax.ShapeDtypeStruct((tokens, dim // n_mp), BF16), jax.ShapeDtypeStruct(grad_shape, F32)),
        in_specs=[smem] * 2 + [pl.BlockSpec(memory_space=pl.ANY)] * 4,
        out_specs=(vmem, vmem),
        scratch_shapes=[
            pltpu.SMEM((tiles,), jnp.int32),
            pltpu.SMEM((n_dp * SLOTS,), jnp.int32),
            pltpu.SMEM((n_dp * SLOTS,), F32),
            pltpu.VMEM((tokens, dim), BF16),
            pltpu.VMEM((hidden, tokens), BF16),
            pltpu.VMEM((tokens, hidden), BF16),
            pltpu.VMEM((hidden, dim), BF16),
            pltpu.VMEM((blocks, block, block), BF16),
            dma((blocks + 3,)),
            pltpu.VMEM((CHUNKS * tiles, rows, LANES), BF16),
            pltpu.VMEM((CHUNKS * tiles, rows, LANES), F32),
            pltpu.VMEM((tiles, rows, LANES), F32),
            pltpu.VMEM((CHUNKS, n_mp, per, rows, LANES), F32),
            pltpu.VMEM((blocks, block, block), BF16),
            pltpu.VMEM((blocks, block, block), BF16),
            pltpu.VMEM((CHUNKS, half_mp, per, rows, LANES), F32),
            pltpu.VMEM((CHUNKS, span, per, rows, LANES), F32),
            pltpu.VMEM((CHUNKS, span, per, rows, LANES), F32),
            pltpu.VMEM((2, ring, width, keep, block), F32),
            pltpu.VMEM((ring, width, keep, block), F32),
            pltpu.VMEM((2, parts, ring // 2, width // parts, keep, block), F32),
            pltpu.VMEM((parts, ring // 2, width // parts, keep, block), F32),
            pltpu.VMEM((parts, ring // 2, width // parts, keep, block), F32),
            pltpu.VMEM((parts, max(ring // 2 - 1, 1), width // parts, keep, block), F32),
            pltpu.VMEM((width, keep, block), F32),
            pltpu.VMEM((span, width, keep, block), F32),
            pltpu.VMEM((width, keep, block), F32),
            pltpu.VMEM((ring, SLOTS, keep, block), F32),
            pltpu.VMEM((ring, SLOTS, keep, block), F32),
            pltpu.VMEM((ring, SLOTS, keep, block), F32),
            dma((CHUNKS, half_mp)), dma((CHUNKS, half_mp)),
            dma((CHUNKS, span)), dma((CHUNKS, span)),
            dma((1,)), dma((1,)),
            dma((parts,)), dma((parts,)),
            dma((parts, max(ring // 2 - 1, 1))), dma((parts, max(ring // 2 - 1, 1))),
            dma((span,)), dma((span,)),
            dma((ring,)), dma((ring,)),
            dma((1,)), dma((1,)),
        ],
        compiler_params=pltpu.CompilerParams(
            collective_id=0, has_side_effects=True, vmem_limit_bytes=62 * 1024 * 1024),
    )(tile_order, block_owner, activations, cotangent.T, frozen_weight.T, skew_params)
    if own_gram:
        return input_grad, grads
    numbers = jnp.arange(blocks, dtype=jnp.int32)
    same = block_owner[:, None] == block_owner[None, :]
    rank = jnp.sum((same & (numbers[:, None] > numbers[None, :])).astype(jnp.int32), axis=1)
    place = block_owner * SLOTS + rank
    chosen = place[None, :] == jnp.arange(n_dp * SLOTS, dtype=jnp.int32)[:, None]
    index = jnp.sum(jnp.where(chosen, numbers[None, :], 0), axis=1)
    valid = jnp.sum(chosen.astype(F32), axis=1)
    gram = lax.psum(grads, ("dp", "mp"))
    at = lax.axis_index("dp") * SLOTS
    mine = lax.dynamic_slice(index, (at,), (SLOTS,))
    used = lax.dynamic_slice(valid, (at,), (SLOTS,))
    g = jnp.take(gram, mine, axis=0) * used[:, None, None]
    plain = jnp.take(skew_params, mine, axis=0).astype(F32)
    qt = jnp.swapaxes(plain, 1, 2) - plain
    mul = functools.partial(jnp.einsum, "bij,bjk->bik", precision=lax.Precision.HIGHEST)
    left = mul(g, qt)
    both = left + mul(qt, g)
    total = 2.0 * g + 2.0 * both + mul(left, qt) + mul(qt, both)
    return input_grad, (total - jnp.swapaxes(total, 1, 2)) * (1.0 / math.sqrt(tokens * n_dp))


def solution(mesh):
    placed = (P("dp", None), P("dp", "mp"), P(None, "mp"), P(), P(), P())
    return jax.shard_map(
        functools.partial(local, mesh.shape["dp"], mesh.shape["mp"]),
        mesh=mesh,
        in_specs=placed,
        out_specs=(P("dp", "mp"), P("dp", None, None)),
        check_vma=False,
    )
```

profile of v0, /device:TPU:0, one launch (start us, length us, event | category | flops | bytes accessed | tf_op | source)
XLA Modules:
  0.0 76.4 jit_solution(12122336015569212139)
XLA Ops:
  0.6 71.7 %shard_map.77 = (bf16[512,640]{1,0:T(8,128)(2,1)}, f32[3,256,256]{2,1,0:T(8,128)}) custom-call(s32[20]{0:T(128)} %order_ref.1, s32[10]{0:T(128)} %owner_ref.1, bf16[512,2560]{1,0:T(8,128)(2,1)} %act_hbm.1, bf16[1728,512]{1,0:T(8,128)(2,1)} %bitcast.3, bf16[1728,2560]{1,0:T(8,128)(2,1)} %bitcast.2, bf16[10,256,256]{2,1,0:T(8,128)(2,1)} %s_hbm.1), custom_call_target="tpu_custom_call" | custom-call | tf_op jit(solution)/shard_map/pallas_call | solution.py:393
  72.3 2.0 %copy.10 = bf16[512,640]{1,0:T(8,128)(2,1)} copy(bf16[512,640]{1,0:T(8,128)(2,1)} %get-tuple-element.4) | data formatting | bytes 1310720
  74.3 2.1 %copy.11 = f32[3,256,256]{2,1,0:T(8,128)} copy(f32[3,256,256]{2,1,0:T(8,128)} %get-tuple-element.5) | data formatting | bytes 1572864
where the time goes:
time: 77.8 us; the launch traced here: 76.4 us
  Pallas kernels  71.7 us (92%)
  local copies, waits for them, and re-layouts  4.04 us (5%)
    pallas_call x1, Pallas kernels, local(): pl.pallas_call(functools.partial(kernel, cfg), out_shape=(jax.ShapeDtypeS...  71.7 us
    unnamed x2, local copies, waits for them, and re-layouts  4.04 us

commit v1 on v0

--- a/solution.py
+++ b/solution.py
@@ -367,6 +367,27 @@
             first(j, o).wait_send()
         for o in range(1, half_mp):
             second(j, o).wait_send()
+
+
+def publish(first, second):
+    def body(a_ref, b_ref, oa_ref, ob_ref, sems):
+        one = pltpu.make_async_copy(a_ref, oa_ref, sems.at[0])
+        two = pltpu.make_async_copy(b_ref, ob_ref, sems.at[1])
+        one.start()
+        two.start()
+        one.wait()
+        two.wait()
+
+    vmem = pl.BlockSpec(memory_space=pltpu.VMEM)
+    hbm = pl.BlockSpec(memory_space=pl.ANY)
+    return pl.pallas_call(
+        body,
+        out_shape=(jax.ShapeDtypeStruct(first.shape, first.dtype), jax.ShapeDtypeStruct(second.shape, second.dtype)),
+        in_specs=[vmem, vmem],
+        out_specs=(hbm, hbm),
+        scratch_shapes=[pltpu.SemaphoreType.DMA((2,))],
+        compiler_params=pltpu.CompilerParams(vmem_limit_bytes=2 * 1024 * 1024),
+    )(first, second)
 
 
 def local(n_dp, n_mp, activations, cotangent, frozen_weight, skew_params, tile_order, block_owner):
@@ -436,10 +457,10 @@
             dma((1,)), dma((1,)),
         ],
         compiler_params=pltpu.CompilerParams(
-            collective_id=0, has_side_effects=True, vmem_limit_bytes=62 * 1024 * 1024),
+            collective_id=0, has_side_effects=True, vmem_limit_bytes=52 * 1024 * 1024),
     )(tile_order, block_owner, activations, cotangent.T, frozen_weight.T, skew_params)
     if own_gram:
-        return input_grad, grads
+        return publish(input_grad, grads)
     numbers = jnp.arange(blocks, dtype=jnp.int32)
     same = block_owner[:, None] == block_owner[None, :]
     rank = jnp.sum((same & (numbers[:, None] > numbers[None, :])).astype(jnp.int32), axis=1)

time: 77.8 us -> 74.8 us (0.961)
  local copies, waits for them, and re-layouts: 4.04 us -> 1.3 us
    unnamed x2 -> x4, local copies, waits for them, and re-layouts: 4.04 us -> 1.3 us
    pallas_call x1, Pallas kernels: 71.7 us -> 70.4 us  [local(): pl.pallas_call(functools.partial(kernel, cfg), out_shape=(jax.ShapeDtypeS...]
    pallas_call x0 -> x1, Pallas kernels: none -> 1.11 us  [publish(): pl.pallas_call(body, out_shape=(jax.ShapeDtypeStruct(first.shape, first.d...]
where the time goes in v1:
time: 74.8 us; the launch traced here: 73.4 us
  Pallas kernels  71.5 us (96%)
  local copies, waits for them, and re-layouts  1.3 us (2%)
    pallas_call x1, Pallas kernels, local(): pl.pallas_call(functools.partial(kernel, cfg), out_shape=(jax.ShapeDtypeS...  70.4 us

profile of v1, /device:TPU:0, one launch (start us, length us, event | category | flops | bytes accessed | tf_op | source)
XLA Modules:
  0.0 73.4 jit_solution(7355248707596578845)
XLA Ops:
  0.6 0.0 copy-start
  0.6 0.6 copy-done
  1.3 0.0 copy-start.1
  1.3 0.7 copy-done.1
  1.9 70.4 %shard_map.77 = (bf16[512,640]{1,0:T(8,128)(2,1)S(1)}, f32[3,256,256]{2,1,0:T(8,128)S(1)}) custom-call(s32[20]{0:T(128)S(1)} %copy-done, s32[10]{0:T(128)S(1)} %copy-done.1, bf16[512,2560]{1,0:T(8,128)(2,1)} %act_hbm.1, bf16[1728,512]{1,0:T(8,128)(2,1)} %bitcast.3, bf16[1728,2560]{1,0:T(8,128)(2,1)} %bitcast.2, bf16[10,256,256]{2,1,0:T(8,128)(2,1)} %s_hbm.1), custom_call_target="tpu_custom_call" | custom-call | tf_op jit(solution)/shard_map/pallas_call | solution.py:414
  72.3 1.1 %shard_map.78 = (bf16[512,640]{1,0:T(8,128)(2,1)}, f32[3,256,256]{2,1,0:T(8,128)}) custom-call(bf16[512,640]{1,0:T(8,128)(2,1)S(1)} %get-tuple-element.4.a_ref, f32[3,256,256]{2,1,0:T(8,128)S(1)} %get-tuple-element.5.b_ref), custom_call_target="tpu_custom_call" | custom-call | tf_op jit(solution)/shard_map/pallas_call | solution.py:383
Async XLA Ops:
  0.6 0.7 copy-start
  1.3 0.7 copy-start.1

commit v2 on v1

v2 whole, which is shorter than its diff:
```python
import functools
import math

import jax
import jax.numpy as jnp
from jax import lax
from jax.experimental import pallas as pl
from jax.experimental.pallas import tpu as pltpu
from jax.sharding import PartitionSpec as P

SLOTS = 3
LANES = 128
MESH = pl.DeviceIdType.MESH
F32 = jnp.float32
BF16 = jnp.bfloat16

NN = (((1,), (0,)), ((), ()))
TN = (((0,), (0,)), ((), ()))


def dot(a, b, dims=NN):
    return lax.dot_general(a, b, dims, preferred_element_type=F32)


def split(x):
    high = x.astype(BF16)
    return high, (x - high.astype(F32)).astype(BF16)


def dot_split(a, b):
    return dot(a[0], b[0]) + (dot(a[0], b[1]) + dot(a[1], b[0]))


def skew_of(params):
    plain = params.astype(F32)
    return plain - plain.T


def cuts(tokens):
    first = tokens * 3 // 8 // 16 * 16
    return ((0, first), (first, tokens)) if first else ((0, tokens),)


def kernel(cfg, order_ref, owner_ref, act_hbm, cot_hbm, w_hbm, s_hbm, out_ref, grad_ref, *scratch):
    tokens, dim, block, blocks, tiles, n_dp, n_mp, own_gram = cfg
    (inv_ref, idx_ref, valid_ref, cot_ref, cots, w_ref, s_ref, acts, feat, outblk, part, recv1, send2, recv2,
     sh, sl, eth, etl, esend, erecv, gsend, gown, grecv, pk, arecv, hsum, zrecv, gp, ax, gfull, slot_out, slot_in,
     lw, la, lo, es, er, s1, r1, s2, r2, gs, gr, xs, xr, ds, dr, ys, yr, ss, sr, ms, mr) = scratch
    half_mp = n_mp // 2
    half = blocks // 2
    per = tiles // n_mp
    chunks = cuts(tokens)
    last = len(chunks) - 1
    dp = lax.axis_index("dp")
    mp = lax.axis_index("mp")
    side = lax.rem(mp, 2)
    group = mp // 2
    mate = group * 2 + (1 - side)

    load_s = pltpu.make_async_copy(s_hbm, s_ref, lo.at[0])
    load_cot = pltpu.make_async_copy(cot_hbm, cot_ref, lo.at[1])

    def load_w(n):
        at = pl.ds(pl.multiple_of(n * block, block), block)
        return pltpu.make_async_copy(w_hbm.at[:, at], w_ref.at[:, at], lw.at[n])

    def load_act(k):
        return pltpu.make_async_copy(act_hbm.at[:, k * LANES:(k + 1) * LANES], acts.at[k], la.at[k])

    load_s.start()
    load_cot.start()
    for n in range(blocks):
        load_w(n).start()
    for k in range(tiles):
        load_act(k).start()

    def same_side(offset):
        return lax.rem(group + offset, half_mp)

    barrier = pltpu.get_barrier_semaphore()
    peers = []
    for o in range(half_mp):
        for k in range(2):
            if o or k:
                peers.append((dp, same_side(o) * 2 + (side if k == 0 else 1 - side)))
    if own_gram:
        for o in range(1, n_dp):
            peers.append((lax.rem(dp + o, n_dp), mp))
        for k in range(2):
            peers.append((dp + 1 - 2 * lax.rem(dp, 2), (1 - group) * 2 + (side if k == 0 else 1 - side)))
    for peer in peers:
        pl.semaphore_signal(barrier, inc=1, device_id=peer, device_id_type=MESH)

    def invert(k, _):
        found = jnp.int32(0)
        for i in range(tiles):
            found = jnp.where(order_ref[i] == k, i, found)
        inv_ref[k] = found
        return 0

    lax.fori_loop(0, tiles, invert, 0)

    def tell(i):
        return pltpu.make_async_remote_copy(
            src_ref=esend.at[i], dst_ref=erecv.at[i], send_sem=es.at[i], recv_sem=er.at[i],
            device_id=(dp, mate), device_id_type=MESH)

    load_s.wait()
    for i in range(half):
        b = side * half + i
        skew = skew_of(s_ref[b])
        pair = split(skew)
        sh[i], sl[i] = pair
        square = dot_split(pair, pair)
        cube = dot_split(split(square), pair)
        turned = 2.0 * square - 2.0 * skew - cube
        esend[i] = turned
        eth[b], etl[b] = split(turned)
    pl.semaphore_wait(barrier, len(peers))
    for i in range(half):
        tell(i).start()

    load_cot.wait()
    for i in range(tokens // LANES):
        cots[i * LANES:(i + 1) * LANES, :] = cot_ref[:, i * LANES:(i + 1) * LANES].T

    def feature(n, at):
        a, z = at
        f = dot(cots[a:z, :], w_ref[:, pl.ds(pl.multiple_of(n * block, block), block)])
        feat[2 * n, a:z] = f[:, :LANES]
        feat[2 * n + 1, a:z] = f[:, LANES:]

    def first_features(k, _):
        for u in range(2):
            load_w(2 * k + u).wait()
        for u in range(2):
            feature(2 * k + u, chunks[0])
        return 0

    def rotate(j):
        a, z = chunks[j]

        def body(k, _):
            for u in range(half):
                b = k * half + u
                f = jnp.concatenate([feat[order_ref[2 * b], a:z], feat[order_ref[2 * b + 1], a:z]], axis=1)
                high, low = split(f)
                out = f + (dot(high, eth[b]) + (dot(low, eth[b]) + dot(high, etl[b])))
                outblk[j][2 * b] = out[:, :LANES]
                outblk[j][2 * b + 1] = out[:, LANES:]
            return 0
        lax.fori_loop(0, 2, body, 0)

    def first(j, o, i):
        q = same_side(o)
        return pltpu.make_async_remote_copy(
            src_ref=part[j].at[q, i], dst_ref=recv1[j].at[q, i],
            send_sem=s1.at[j, o, i], recv_sem=r1.at[j, o, i],
            device_id=(dp, mate), device_id_type=MESH)

    def second(j, o, i):
        return pltpu.make_async_remote_copy(
            src_ref=send2[j].at[o - 1, i], dst_ref=recv2[j].at[o - 1, i],
            send_sem=s2.at[j, o - 1, i], recv_sem=r2.at[j, o - 1, i],
            device_id=(dp, same_side(o) * 2 + side), device_id_type=MESH)

    def start_first(j):
        for o in list(range(1, half_mp)) + [0]:
            q = same_side(o)
            for i in range(per):
                part[j][q, i] = outblk[j][inv_ref[(q * 2 + (1 - side)) * per + i]]
                first(j, o, i).start()

    def start_second(j):
        for o in range(1, half_mp):
            q = same_side(o)
            for i in range(per):
                first(j, o, i).wait_recv()
                send2[j][o - 1, i] = outblk[j][inv_ref[(q * 2 + side) * per + i]] + recv1[j][q, i]
                second(j, o, i).start()

    def finish(j):
        a, z = chunks[j]
        for i in range(per):
            first(j, 0, i).wait_recv()
            total = outblk[j][inv_ref[mp * per + i]] + recv1[j][group, i]
            for o in range(1, half_mp):
                second(j, o, i).wait_recv()
                total = total + recv2[j][o - 1, i]
            out_ref[a:z, i * LANES:(i + 1) * LANES] = total.astype(out_ref.dtype)

    def gram_of(b):
        t0 = order_ref[2 * b]
        t1 = order_ref[2 * b + 1]
        high, low = split(jnp.concatenate([feat[t0], feat[t1]], axis=1))
        x = jnp.concatenate([acts[t0], acts[t1]], axis=1)
        return dot(x, high, TN) + dot(x, low, TN)

    def swap(i):
        return pltpu.make_async_remote_copy(
            src_ref=gsend.at[i], dst_ref=grecv.at[i], send_sem=gs.at[i], recv_sem=gr.at[i],
            device_id=(dp, mate), device_id_type=MESH)

    lax.fori_loop(0, blocks // 2, first_features, 0)
    for i in range(half):
        tell(i).wait_recv()
        b = (1 - side) * half + i
        eth[b], etl[b] = split(erecv[i])
    rotate(0)
    start_first(0)
    for j in range(1, last + 1):
        for n in range(half):
            feature(n, chunks[j])
        start_second(j - 1)
        for n in range(half, blocks):
            feature(n, chunks[j])
    for k in range(tiles):
        load_act(k).wait()

    if own_gram:
        parity = lax.rem(dp, 2)
        line = dp // 2
        n_line = n_dp // 2
        piece = block // 2 // n_dp
        mine = lax.rem(parity + group, 2)
        across = dp + 1 - 2 * parity

        def cross(i):
            return pltpu.make_async_remote_copy(
                src_ref=pk.at[i, 1 - mine], dst_ref=arecv.at[i], send_sem=xs.at[i], recv_sem=xr.at[i],
                device_id=(across, mp), device_id_type=MESH)

        def along(i, o):
            to = lax.rem(line + o, n_line)
            return pltpu.make_async_remote_copy(
                src_ref=hsum.at[i, to], dst_ref=zrecv.at[i, o - 1],
                send_sem=ds.at[i, o - 1], recv_sem=dr.at[i, o - 1],
                device_id=(to * 2 + parity, mp), device_id_type=MESH)

        def trade(k):
            column = side if k == 1 else 1 - side
            to = (dp, mate) if k == 0 else (across, (1 - group) * 2 + column)
            return pltpu.make_async_remote_copy(
                src_ref=gp.at[column], dst_ref=ax.at[k], send_sem=ys.at[k], recv_sem=yr.at[k],
                device_id=to, device_id_type=MESH)

        def deliver(o):
            to = lax.rem(dp + o, n_dp)
            return pltpu.make_async_remote_copy(
                src_ref=slot_out.at[to], dst_ref=slot_in.at[side, dp],
                send_sem=ss.at[o], recv_sem=sr.at[o],
                device_id=(to, mp), device_id_type=MESH)

        share = pltpu.make_async_remote_copy(
            src_ref=slot_in.at[side], dst_ref=slot_in.at[side], send_sem=ms.at[0], recv_sem=mr.at[0],
            device_id=(dp, mate), device_id_type=MESH)

        row = lax.broadcasted_iota(jnp.int32, (LANES, LANES), 0)
        column = lax.broadcasted_iota(jnp.int32, (LANES, LANES), 1)

        for i in range(half):
            gsend[i] = gram_of((1 - side) * half + i)
            swap(i).start()
        for i in range(half):
            gown[i] = gram_of(side * half + i)
        for i in range(half):
            swap(i).wait_recv()
        for i in range(half):
            g = gown[i] + grecv[i]
            turned = g.T
            odd = g - turned
            pair = (sh[i], sl[i])
            once = dot_split(split(odd), pair)
            twice = dot_split(split(2.0 * (g + turned) - once - 0.5 * once.T), pair)
            x = odd - twice
            upper = x[:LANES, :LANES]
            lower = x[LANES:, LANES:]
            corner = jnp.where(row < column, upper - upper.T, lower - lower.T)
            packed = jnp.concatenate([corner, x[:LANES, LANES:] - x[LANES:, :LANES].T], axis=1)
            for h in range(2):
                for q in range(n_line):
                    at = (h * n_line + q) * piece
                    pk[i, h, q] = packed[at:at + piece]
        for i in range(half):
            cross(i).start()
    else:
        for b in range(blocks):
            grad_ref[b] = gram_of(b)

    if last:
        rotate(last)
        start_first(last)
    start_second(last)

    if own_gram:
        for i in range(half):
            cross(i).wait_recv()
            hsum[i] = pk[i, mine] + arecv[i]
            for o in range(1, n_line):
                along(i, o).start()

        places = []
        for b in range(blocks):
            place = owner_ref[b] * SLOTS
            for e in range(b):
                place = place + jnp.where(owner_ref[e] == owner_ref[b], 1, 0)
            places.append(place)

        def locate(q, _):
            found = jnp.int32(0)
            count = jnp.float32(0.0)
            for b in range(blocks):
                found = jnp.where(places[b] == q, b, found)
                count = jnp.where(places[b] == q, 1.0, count)
            idx_ref[q] = found
            valid_ref[q] = count
            return 0

        lax.fori_loop(0, n_dp * SLOTS, locate, 0)

        for i in range(half):
            total = hsum[i, line]
            for o in range(1, n_line):
                along(i, o).wait_recv()
                total = total + zrecv[i, o - 1]
            for h in range(2):
                gp[h, i] = total[:, h * LANES:(h + 1) * LANES]
        for k in range(3):
            trade(k).start()
        for k in range(3):
            trade(k).wait_recv()
        for i in range(half):
            gfull[side * half + i] = gp[side, i] + ax[1, i]
            gfull[(1 - side) * half + i] = ax[0, i] + ax[2, i]
        for d in range(n_dp):
            for s in range(SLOTS):
                slot_out[d, s] = gfull[idx_ref[d * SLOTS + s]] * valid_ref[d * SLOTS + s]
        for o in range(1, n_dp):
            deliver(o).start()
        slot_in[side, dp] = slot_out[dp]
        for j in range(last):
            finish(j)
        for o in range(1, n_dp):
            deliver(o).wait_recv()
        share.start()
        share.wait_recv()
        scale = 1.0 / math.sqrt(tokens * n_dp)
        for s in range(SLOTS):
            whole = []
            for h in range(2):
                rows = []
                for p in range(n_dp):
                    source = 2 * (p % n_line) + lax.rem(p // n_line + group, 2)
                    rows.append(slot_in[h, source, s])
                whole.append(jnp.concatenate(rows, axis=0) * scale)
            corner, beside = whole
            upper = jnp.where(row < column, corner, 0.0)
            lower = jnp.where(row > column, corner, 0.0)
            grad_ref[s, :LANES, :LANES] = upper - upper.T
            grad_ref[s, LANES:, LANES:] = lower - lower.T
            grad_ref[s, :LANES, LANES:] = beside
            grad_ref[s, LANES:, :LANES] = -beside.T
        finish(last)
        for i in range(half):
            swap(i).wait_send()
            cross(i).wait_send()
            for o in range(1, n_line):
                along(i, o).wait_send()
        for k in range(3):
            trade(k).wait_send()
        for o in range(1, n_dp):
            deliver(o).wait_send()
        share.wait_send()
    else:
        for j in range(last + 1):
            finish(j)
    for i in range(half):
        tell(i).wait_send()
    for j in range(last + 1):
        for i in range(per):
            for o in range(half_mp):
                first(j, o, i).wait_send()
            for o in range(1, half_mp):
                second(j, o, i).wait_send()


def publish(first, second):
    def body(a_ref, b_ref, oa_ref, ob_ref, sems):
        one = pltpu.make_async_copy(a_ref, oa_ref, sems.at[0])
        two = pltpu.make_async_copy(b_ref, ob_ref, sems.at[1])
        one.start()
        two.start()
        one.wait()
        two.wait()

    vmem = pl.BlockSpec(memory_space=pltpu.VMEM)
    hbm = pl.BlockSpec(memory_space=pl.ANY)
    return pl.pallas_call(
        body,
        out_shape=(jax.ShapeDtypeStruct(first.shape, first.dtype), jax.ShapeDtypeStruct(second.shape, second.dtype)),
        in_specs=[vmem, vmem],
        out_specs=(hbm, hbm),
        scratch_shapes=[pltpu.SemaphoreType.DMA((2,))],
        compiler_params=pltpu.CompilerParams(vmem_limit_bytes=2 * 1024 * 1024),
    )(first, second)


def local(n_dp, n_mp, activations, cotangent, frozen_weight, skew_params, tile_order, block_owner):
    tokens, dim = activations.shape
    hidden = cotangent.shape[1]
    blocks, block, _ = skew_params.shape
    tiles = tile_order.shape[0]
    piece = block // 2 // n_dp
    own_gram = piece * n_dp * 2 == block and piece % 8 == 0 and n_dp % 2 == 0 and n_mp == 4 and block == 2 * LANES
    keep = piece if own_gram else 8
    ring = n_dp if own_gram else 2
    half = blocks // 2
    some = half if own_gram else 1
    n_line = ring // 2
    half_mp = n_mp // 2
    per = tiles // n_mp
    span = max(half_mp - 1, 1)
    sizes = [z - a for a, z in cuts(tokens)]
    count = len(sizes)

    cfg = (tokens, dim, block, blocks, tiles, n_dp, n_mp, own_gram)
    smem = pl.BlockSpec(memory_space=pltpu.SMEM)
    vmem = pl.BlockSpec(memory_space=pltpu.VMEM)
    dma = pltpu.SemaphoreType.DMA
    grad_shape = (SLOTS if own_gram else blocks, block, block)
    squares = pltpu.VMEM((half, block, block), F32)
    gram = pltpu.VMEM((some, block, block), F32)

    def by_chunk(*lead):
        return tuple(pltpu.VMEM((*lead, rows, LANES), F32) for rows in sizes)

    input_grad, grads = pl.pallas_call(
        functools.partial(kernel, cfg),
        out_shape=(jax.ShapeDtypeStruct((tokens, dim // n_mp), BF16), jax.ShapeDtypeStruct(grad_shape, F32)),
        in_specs=[smem] * 2 + [pl.BlockSpec(memory_space=pl.ANY)] * 4,
        out_specs=(vmem, vmem),
        scratch_shapes=[
            pltpu.SMEM((tiles,), jnp.int32),
            pltpu.SMEM((n_dp * SLOTS,), jnp.int32),
            pltpu.SMEM((n_dp * SLOTS,), F32),
            pltpu.VMEM((hidden, tokens), BF16),
            pltpu.VMEM((tokens, hidden), BF16),
            pltpu.VMEM((hidden, dim), BF16),
            pltpu.VMEM((blocks, block, block), BF16),
            pltpu.VMEM((tiles, tokens, LANES), BF16),
            pltpu.VMEM((tiles, tokens, LANES), F32),
            by_chunk(tiles),
            by_chunk(half_mp, per),
            by_chunk(half_mp, per),
            by_chunk(span, per),
            by_chunk(span, per),
            pltpu.VMEM((half, block, block), BF16),
            pltpu.VMEM((half, block, block), BF16),
            pltpu.VMEM((blocks, block, block), BF16),
            pltpu.VMEM((blocks, block, block), BF16),
            squares, squares,
            gram, gram, gram,
            pltpu.VMEM((some, 2, n_line, keep, block), F32),
            pltpu.VMEM((some, n_line, keep, block), F32),
            pltpu.VMEM((some, n_line, keep, block), F32),
            pltpu.VMEM((some, max(n_line - 1, 1), keep, block), F32),
            pltpu.VMEM((2, some, keep, LANES), F32),
            pltpu.VMEM((3, some, keep, LANES), F32),
            pltpu.VMEM((2 * some, keep, LANES), F32),
            pltpu.VMEM((ring, SLOTS, keep, LANES), F32),
            pltpu.VMEM((2, ring, SLOTS, keep, LANES), F32),
            dma((blocks,)), dma((tiles,)), dma((2,)),
            dma((half,)), dma((half,)),
            dma((count, half_mp, per)), dma((count, half_mp, per)),
            dma((count, span, per)), dma((count, span, per)),
            dma((half,)), dma((half,)),
            dma((half,)), dma((half,)),
            dma((half, max(n_line - 1, 1))), dma((half, max(n_line - 1, 1))),
            dma((3,)), dma((3,)),
            dma((ring,)), dma((ring,)),
            dma((1,)), dma((1,)),
        ],
        compiler_params=pltpu.CompilerParams(
            collective_id=0, has_side_effects=True, vmem_limit_bytes=54 * 1024 * 1024),
    )(tile_order, block_owner, activations, cotangent.T, frozen_weight.T, skew_params)
    if own_gram:
        return publish(input_grad, grads)
    numbers = jnp.arange(blocks, dtype=jnp.int32)
    same = block_owner[:, None] == block_owner[None, :]
    rank = jnp.sum((same & (numbers[:, None] > numbers[None, :])).astype(jnp.int32), axis=1)
    place = block_owner * SLOTS + rank
    chosen = place[None, :] == jnp.arange(n_dp * SLOTS, dtype=jnp.int32)[:, None]
    index = jnp.sum(jnp.where(chosen, numbers[None, :], 0), axis=1)
    valid = jnp.sum(chosen.astype(F32), axis=1)
    gram = lax.psum(grads, ("dp", "mp"))
    at = lax.axis_index("dp") * SLOTS
    mine = lax.dynamic_slice(index, (at,), (SLOTS,))
    used = lax.dynamic_slice(valid, (at,), (SLOTS,))
    g = jnp.take(gram, mine, axis=0) * used[:, None, None]
    plain = jnp.take(skew_params, mine, axis=0).astype(F32)
    qt = jnp.swapaxes(plain, 1, 2) - plain
    mul = functools.partial(jnp.einsum, "bij,bjk->bik", precision=lax.Precision.HIGHEST)
    left = mul(g, qt)
    both = left + mul(qt, g)
    total = 2.0 * g + 2.0 * both + mul(left, qt) + mul(qt, both)
    return input_grad, (total - jnp.swapaxes(total, 1, 2)) * (1.0 / math.sqrt(tokens * n_dp))


def solution(mesh):
    placed = (P("dp", None), P("dp", "mp"), P(None, "mp"), P(), P(), P())
    return jax.shard_map(
        functools.partial(local, mesh.shape["dp"], mesh.shape["mp"]),
        mesh=mesh,
        in_specs=placed,
        out_specs=(P("dp", "mp"), P("dp", None, None)),
        check_vma=False,
    )
```

time: 74.8 us -> 54.5 us (0.73); the launches traced: 73.4 us -> 54 us
  Pallas kernels: 71.5 us -> 51.1 us
  local copies, waits for them, and re-layouts: 1.3 us -> 2.21 us
    pallas_call x1, Pallas kernels: 70.4 us -> 50 us  [local(): pl.pallas_call(functools.partial(kernel, cfg), out_shape=(jax.ShapeDtypeS...]
    unnamed x4, local copies, waits for them, and re-layouts: 1.3 us -> 2.21 us
where the time goes in v2:
time: 54.5 us; the launch traced here: 54 us
  Pallas kernels  51.1 us (94%)
  local copies, waits for them, and re-layouts  2.21 us (4%)
  between operations  0.65 us (1%)
    pallas_call x1, Pallas kernels, local(): pl.pallas_call(functools.partial(kernel, cfg), out_shape=(jax.ShapeDtypeS...  50 us
    unnamed x4, local copies, waits for them, and re-layouts  2.21 us
    pallas_call x1, Pallas kernels, publish(): pl.pallas_call(body, out_shape=(jax.ShapeDtypeStruct(first.shape, first.d...  1.11 us

profile of v2, /device:TPU:0, one launch (start us, length us, event | category | flops | bytes accessed | tf_op | source)
XLA Modules:
  0.0 54.0 jit_solution(2143797016827174005)
XLA Ops:
  0.6 50.0 %shard_map.77 = (bf16[512,640]{1,0:T(8,128)(2,1)}, f32[3,256,256]{2,1,0:T(8,128)}) custom-call(s32[20]{0:T(128)} %order_ref.1, s32[10]{0:T(128)} %owner_ref.1, bf16[512,2560]{1,0:T(8,128)(2,1)} %act_hbm.1, bf16[1728,512]{1,0:T(8,128)(2,1)} %bitcast.3, bf16[1728,2560]{1,0:T(8,128)(2,1)} %bitcast.2, bf16[10,256,256]{2,1,0:T(8,128)(2,1)} %s_hbm.1), custom_call_target="tpu_custom_call" | custom-call | tf_op jit(solution)/shard_map/pallas_call | solution.py:437
  50.6 0.0 copy-start
  50.6 1.1 %copy-done = f32[3,256,256]{2,1,0:T(8,128)S(1)} copy-done((f32[3,256,256]{2,1,0:T(8,128)S(1)}, f32[3,256,256]{2,1,0:T(8,128)}, u32[]{:S(2)}) %copy-start) | copy-done | bytes 786456
  51.8 0.0 copy-start.1
  51.8 1.1 %copy-done.1 = bf16[512,640]{1,0:T(8,128)(2,1)S(1)} copy-done((bf16[512,640]{1,0:T(8,128)(2,1)S(1)}, bf16[512,640]{1,0:T(8,128)(2,1)}, u32[]{:S(2)}) %copy-start.1) | copy-done | bytes 655384
  52.8 1.1 %shard_map.78 = (bf16[512,640]{1,0:T(8,128)(2,1)}, f32[3,256,256]{2,1,0:T(8,128)}) custom-call(bf16[512,640]{1,0:T(8,128)(2,1)S(1)} %copy-done.1, f32[3,256,256]{2,1,0:T(8,128)S(1)} %copy-done), custom_call_target="tpu_custom_call" | custom-call | tf_op jit(solution)/shard_map/pallas_call | solution.py:398
Async XLA Ops:
  50.6 1.1 %copy-start = (f32[3,256,256]{2,1,0:T(8,128)S(1)}, f32[3,256,256]{2,1,0:T(8,128)}, u32[]{:S(2)}) copy-start(f32[3,256,256]{2,1,0:T(8,128)} %get-tuple-element.5.b_ref) | copy-start | bytes 2359300
  51.8 1.1 %copy-start.1 = (bf16[512,640]{1,0:T(8,128)(2,1)S(1)}, bf16[512,640]{1,0:T(8,128)(2,1)}, u32[]{:S(2)}) copy-start(bf16[512,640]{1,0:T(8,128)(2,1)} %get-tuple-element.4.a_ref) | copy-start | bytes 1966084

commit v3 on v2

--- a/solution.py
+++ b/solution.py
@@ -9,6 +9,7 @@
 from jax.sharding import PartitionSpec as P
 
 SLOTS = 3
+AHEAD = 4
 LANES = 128
 MESH = pl.DeviceIdType.MESH
 F32 = jnp.float32
@@ -41,9 +42,9 @@
     return ((0, first), (first, tokens)) if first else ((0, tokens),)
 
 
-def kernel(cfg, order_ref, owner_ref, act_hbm, cot_hbm, w_hbm, s_hbm, out_ref, grad_ref, *scratch):
+def kernel(cfg, order_hbm, owner_hbm, act_hbm, cot_hbm, w_hbm, s_hbm, out_ref, grad_ref, *scratch):
     tokens, dim, block, blocks, tiles, n_dp, n_mp, own_gram = cfg
-    (inv_ref, idx_ref, valid_ref, cot_ref, cots, w_ref, s_ref, acts, feat, outblk, part, recv1, send2, recv2,
+    (order_ref, owner_ref, inv_ref, idx_ref, valid_ref, cot_ref, cots, w_ref, s_ref, acts, feat, outblk, part, recv1, send2, recv2,
      sh, sl, eth, etl, esend, erecv, gsend, gown, grecv, pk, arecv, hsum, zrecv, gp, ax, gfull, slot_out, slot_in,
      lw, la, lo, es, er, s1, r1, s2, r2, gs, gr, xs, xr, ds, dr, ys, yr, ss, sr, ms, mr) = scratch
     half_mp = n_mp // 2
@@ -67,12 +68,14 @@
     def load_act(k):
         return pltpu.make_async_copy(act_hbm.at[:, k * LANES:(k + 1) * LANES], acts.at[k], la.at[k])
 
+    load_order = pltpu.make_async_copy(order_hbm, order_ref, lo.at[2])
+    load_owner = pltpu.make_async_copy(owner_hbm, owner_ref, lo.at[3])
     load_s.start()
+    load_order.start()
+    load_owner.start()
     load_cot.start()
-    for n in range(blocks):
+    for n in range(AHEAD):
         load_w(n).start()
-    for k in range(tiles):
-        load_act(k).start()
 
     def same_side(offset):
         return lax.rem(group + offset, half_mp)
@@ -98,6 +101,8 @@
         inv_ref[k] = found
         return 0
 
+    load_order.wait()
+    load_owner.wait()
     lax.fori_loop(0, tiles, invert, 0)
 
     def tell(i):
@@ -119,6 +124,10 @@
     pl.semaphore_wait(barrier, len(peers))
     for i in range(half):
         tell(i).start()
+    for n in range(AHEAD, blocks):
+        load_w(n).start()
+    for k in range(tiles):
+        load_act(k).start()
 
     load_cot.wait()
     for i in range(tokens // LANES):
@@ -424,7 +433,6 @@
     count = len(sizes)
 
     cfg = (tokens, dim, block, blocks, tiles, n_dp, n_mp, own_gram)
-    smem = pl.BlockSpec(memory_space=pltpu.SMEM)
     vmem = pl.BlockSpec(memory_space=pltpu.VMEM)
     dma = pltpu.SemaphoreType.DMA
     grad_shape = (SLOTS if own_gram else blocks, block, block)
@@ -437,9 +445,11 @@
     input_grad, grads = pl.pallas_call(
         functools.partial(kernel, cfg),
         out_shape=(jax.ShapeDtypeStruct((tokens, dim // n_mp), BF16), jax.ShapeDtypeStruct(grad_shape, F32)),
-        in_specs=[smem] * 2 + [pl.BlockSpec(memory_space=pl.ANY)] * 4,
+        in_specs=[pl.BlockSpec(memory_space=pltpu.HBM)] * 2 + [pl.BlockSpec(memory_space=pl.ANY)] * 4,
         out_specs=(vmem, vmem),
         scratch_shapes=[
+            pltpu.SMEM((tiles,), jnp.int32),
+            pltpu.SMEM((blocks,), jnp.int32),
             pltpu.SMEM((tiles,), jnp.int32),
             pltpu.SMEM((n_dp * SLOTS,), jnp.int32),
             pltpu.SMEM((n_dp * SLOTS,), F32),
@@ -469,7 +479,7 @@
             pltpu.VMEM((2 * some, keep, LANES), F32),
             pltpu.VMEM((ring, SLOTS, keep, LANES), F32),
             pltpu.VMEM((2, ring, SLOTS, keep, LANES), F32),
-            dma((blocks,)), dma((tiles,)), dma((2,)),
+            dma((blocks,)), dma((tiles,)), dma((4,)),
             dma((half,)), dma((half,)),
             dma((count, half_mp, per)), dma((count, half_mp, per)),
             dma((count, span, per)), dma((count, span, per)),

time: 54.5 us -> 52.2 us (0.958)
  Pallas kernels: 51.1 us -> 49.2 us
    pallas_call x1, Pallas kernels: 50 us -> 48 us  [local(): pl.pallas_call(functools.partial(kernel, cfg), out_shape=(jax.ShapeDtypeS...]
where the time goes in v3:
time: 52.2 us; the launch traced here: 52 us
  Pallas kernels  49.2 us (94%)
  local copies, waits for them, and re-layouts  2.21 us (4%)
  between operations  0.65 us (1%)
    pallas_call x1, Pallas kernels, local(): pl.pallas_call(functools.partial(kernel, cfg), out_shape=(jax.ShapeDtypeS...  48 us
    unnamed x4, local copies, waits for them, and re-layouts  2.21 us
    pallas_call x1, Pallas kernels, publish(): pl.pallas_call(body, out_shape=(jax.ShapeDtypeStruct(first.shape, first.d...  1.11 us

profile of v3, /device:TPU:0, one launch (start us, length us, event | category | flops | bytes accessed | tf_op | source)
XLA Modules:
  0.0 52.0 jit_solution(8431712729084082498)
XLA Ops:
  0.6 48.0 %shard_map.77 = (bf16[512,640]{1,0:T(8,128)(2,1)}, f32[3,256,256]{2,1,0:T(8,128)}) custom-call(s32[20]{0:T(128)} %order_hbm.1, s32[10]{0:T(128)} %owner_hbm.1, bf16[512,2560]{1,0:T(8,128)(2,1)} %act_hbm.1, bf16[1728,512]{1,0:T(8,128)(2,1)} %bitcast.3, bf16[1728,2560]{1,0:T(8,128)(2,1)} %bitcast.2, bf16[10,256,256]{2,1,0:T(8,128)(2,1)} %s_hbm.1), custom_call_target="tpu_custom_call" | custom-call | tf_op jit(solution)/shard_map/pallas_call | solution.py:445
  48.7 0.0 copy-start
  48.7 1.1 %copy-done = f32[3,256,256]{2,1,0:T(8,128)S(1)} copy-done((f32[3,256,256]{2,1,0:T(8,128)S(1)}, f32[3,256,256]{2,1,0:T(8,128)}, u32[]{:S(2)}) %copy-start) | copy-done | bytes 786456
  49.8 0.0 copy-start.1
  49.8 1.1 %copy-done.1 = bf16[512,640]{1,0:T(8,128)(2,1)S(1)} copy-done((bf16[512,640]{1,0:T(8,128)(2,1)S(1)}, bf16[512,640]{1,0:T(8,128)(2,1)}, u32[]{:S(2)}) %copy-start.1) | copy-done | bytes 655384
  50.9 1.1 %shard_map.78 = (bf16[512,640]{1,0:T(8,128)(2,1)}, f32[3,256,256]{2,1,0:T(8,128)}) custom-call(bf16[512,640]{1,0:T(8,128)(2,1)S(1)} %copy-done.1, f32[3,256,256]{2,1,0:T(8,128)S(1)} %copy-done), custom_call_target="tpu_custom_call" | custom-call | tf_op jit(solution)/shard_map/pallas_call | solution.py:407
Async XLA Ops:
  48.7 1.1 %copy-start = (f32[3,256,256]{2,1,0:T(8,128)S(1)}, f32[3,256,256]{2,1,0:T(8,128)}, u32[]{:S(2)}) copy-start(f32[3,256,256]{2,1,0:T(8,128)} %get-tuple-element.5.b_ref) | copy-start | bytes 2359300
  49.8 1.1 %copy-start.1 = (bf16[512,640]{1,0:T(8,128)(2,1)S(1)}, bf16[512,640]{1,0:T(8,128)(2,1)}, u32[]{:S(2)}) copy-start(bf16[512,640]{1,0:T(8,128)(2,1)} %get-tuple-element.4.a_ref) | copy-start | bytes 1966084

commit v4 on v2

--- a/solution.py
+++ b/solution.py
@@ -9,6 +9,7 @@
 from jax.sharding import PartitionSpec as P
 
 SLOTS = 3
+AHEAD = 4
 LANES = 128
 MESH = pl.DeviceIdType.MESH
 F32 = jnp.float32
@@ -41,7 +42,7 @@
     return ((0, first), (first, tokens)) if first else ((0, tokens),)
 
 
-def kernel(cfg, order_ref, owner_ref, act_hbm, cot_hbm, w_hbm, s_hbm, out_ref, grad_ref, *scratch):
+def kernel(cfg, index_ref, act_hbm, cot_hbm, w_hbm, s_hbm, out_ref, grad_ref, *scratch):
     tokens, dim, block, blocks, tiles, n_dp, n_mp, own_gram = cfg
     (inv_ref, idx_ref, valid_ref, cot_ref, cots, w_ref, s_ref, acts, feat, outblk, part, recv1, send2, recv2,
      sh, sl, eth, etl, esend, erecv, gsend, gown, grecv, pk, arecv, hsum, zrecv, gp, ax, gfull, slot_out, slot_in,
@@ -69,10 +70,8 @@
 
     load_s.start()
     load_cot.start()
-    for n in range(blocks):
+    for n in range(AHEAD):
         load_w(n).start()
-    for k in range(tiles):
-        load_act(k).start()
 
     def same_side(offset):
         return lax.rem(group + offset, half_mp)
@@ -94,9 +93,10 @@
     def invert(k, _):
         found = jnp.int32(0)
         for i in range(tiles):
-            found = jnp.where(order_ref[i] == k, i, found)
+            found = jnp.where(index_ref[i] == k, i, found)
         inv_ref[k] = found
         return 0
+
 
     lax.fori_loop(0, tiles, invert, 0)
 
@@ -119,6 +119,10 @@
     pl.semaphore_wait(barrier, len(peers))
     for i in range(half):
         tell(i).start()
+    for n in range(AHEAD, blocks):
+        load_w(n).start()
+    for k in range(tiles):
+        load_act(k).start()
 
     load_cot.wait()
     for i in range(tokens // LANES):
@@ -143,7 +147,7 @@
         def body(k, _):
             for u in range(half):
                 b = k * half + u
-                f = jnp.concatenate([feat[order_ref[2 * b], a:z], feat[order_ref[2 * b + 1], a:z]], axis=1)
+                f = jnp.concatenate([feat[index_ref[2 * b], a:z], feat[index_ref[2 * b + 1], a:z]], axis=1)
                 high, low = split(f)
                 out = f + (dot(high, eth[b]) + (dot(low, eth[b]) + dot(high, etl[b])))
                 outblk[j][2 * b] = out[:, :LANES]
@@ -190,8 +194,8 @@
             out_ref[a:z, i * LANES:(i + 1) * LANES] = total.astype(out_ref.dtype)
 
     def gram_of(b):
-        t0 = order_ref[2 * b]
-        t1 = order_ref[2 * b + 1]
+        t0 = index_ref[2 * b]
+        t1 = index_ref[2 * b + 1]
         high, low = split(jnp.concatenate([feat[t0], feat[t1]], axis=1))
         x = jnp.concatenate([acts[t0], acts[t1]], axis=1)
         return dot(x, high, TN) + dot(x, low, TN)
@@ -237,11 +241,11 @@
                 send_sem=ds.at[i, o - 1], recv_sem=dr.at[i, o - 1],
                 device_id=(to * 2 + parity, mp), device_id_type=MESH)
 
-        def trade(k):
+        def trade(k, i):
             column = side if k == 1 else 1 - side
             to = (dp, mate) if k == 0 else (across, (1 - group) * 2 + column)
             return pltpu.make_async_remote_copy(
-                src_ref=gp.at[column], dst_ref=ax.at[k], send_sem=ys.at[k], recv_sem=yr.at[k],
+                src_ref=gp.at[column, i], dst_ref=ax.at[k, i], send_sem=ys.at[k, i], recv_sem=yr.at[k, i],
                 device_id=to, device_id_type=MESH)
 
         def deliver(o):
@@ -301,9 +305,9 @@
 
         places = []
         for b in range(blocks):
-            place = owner_ref[b] * SLOTS
+            place = index_ref[tiles + b] * SLOTS
             for e in range(b):
-                place = place + jnp.where(owner_ref[e] == owner_ref[b], 1, 0)
+                place = place + jnp.where(index_ref[tiles + e] == index_ref[tiles + b], 1, 0)
             places.append(place)
 
         def locate(q, _):
@@ -325,10 +329,11 @@
                 total = total + zrecv[i, o - 1]
             for h in range(2):
                 gp[h, i] = total[:, h * LANES:(h + 1) * LANES]
-        for k in range(3):
-            trade(k).start()
-        for k in range(3):
-            trade(k).wait_recv()
+            for k in range(3):
+                trade(k, i).start()
+        for i in range(half):
+            for k in range(3):
+                trade(k, i).wait_recv()
         for i in range(half):
             gfull[side * half + i] = gp[side, i] + ax[1, i]
             gfull[(1 - side) * half + i] = ax[0, i] + ax[2, i]
@@ -366,8 +371,8 @@
             cross(i).wait_send()
             for o in range(1, n_line):
                 along(i, o).wait_send()
-        for k in range(3):
-            trade(k).wait_send()
+            for k in range(3):
+                trade(k, i).wait_send()
         for o in range(1, n_dp):
             deliver(o).wait_send()
         share.wait_send()
@@ -424,7 +429,6 @@
     count = len(sizes)
 
     cfg = (tokens, dim, block, blocks, tiles, n_dp, n_mp, own_gram)
-    smem = pl.BlockSpec(memory_space=pltpu.SMEM)
     vmem = pl.BlockSpec(memory_space=pltpu.VMEM)
     dma = pltpu.SemaphoreType.DMA
     grad_shape = (SLOTS if own_gram else blocks, block, block)
@@ -437,7 +441,7 @@
     input_grad, grads = pl.pallas_call(
         functools.partial(kernel, cfg),
         out_shape=(jax.ShapeDtypeStruct((tokens, dim // n_mp), BF16), jax.ShapeDtypeStruct(grad_shape, F32)),
-        in_specs=[smem] * 2 + [pl.BlockSpec(memory_space=pl.ANY)] * 4,
+        in_specs=[pl.BlockSpec(memory_space=pltpu.SMEM)] + [pl.BlockSpec(memory_space=pl.ANY)] * 4,
         out_specs=(vmem, vmem),
         scratch_shapes=[
             pltpu.SMEM((tiles,), jnp.int32),
@@ -476,13 +480,13 @@
             dma((half,)), dma((half,)),
             dma((half,)), dma((half,)),
             dma((half, max(n_line - 1, 1))), dma((half, max(n_line - 1, 1))),
-            dma((3,)), dma((3,)),
+            dma((3, half)), dma((3, half)),
             dma((ring,)), dma((ring,)),
             dma((1,)), dma((1,)),
         ],
         compiler_params=pltpu.CompilerParams(
-            collective_id=0, has_side_effects=True, vmem_limit_bytes=54 * 1024 * 1024),
-    )(tile_order, block_owner, activations, cotangent.T, frozen_weight.T, skew_params)
+            collective_id=0, has_side_effects=True, vmem_limit_bytes=52 * 1024 * 1024),
+    )(jnp.concatenate([tile_order, block_owner]), activations, cotangent.T, frozen_weight.T, skew_params)
     if own_gram:
         return publish(input_grad, grads)
     numbers = jnp.arange(blocks, dtype=jnp.int32)

time: 54.5 us -> 50.3 us (0.923)
  Pallas kernels: 51.1 us -> 48.8 us
  local copies, waits for them, and re-layouts: 2.21 us -> 0 us
  other arithmetic: 0 us -> 0.75 us
    pallas_call x1, Pallas kernels: 50 us -> 47.7 us  [local(): pl.pallas_call(functools.partial(kernel, cfg), out_shape=(jax.ShapeDtypeS...]
    unnamed x4 -> x0, local copies, waits for them, and re-layouts: 2.21 us -> none
    concatenate x0 -> x1, other arithmetic: none -> 0.75 us  [local(): jnp.concatenate([tile_order, block_owner])]
where the time goes in v4:
time: 50.3 us; the launch traced here: 50.2 us
  Pallas kernels  48.8 us (97%)
  other arithmetic  0.75 us (1%)
  between operations  0.64 us (1%)
    pallas_call x1, Pallas kernels, local(): pl.pallas_call(functools.partial(kernel, cfg), out_shape=(jax.ShapeDtypeS...  47.7 us
    pallas_call x1, Pallas kernels, publish(): pl.pallas_call(body, out_shape=(jax.ShapeDtypeStruct(first.shape, first.d...  1.11 us

profile of v4, /device:TPU:0, one launch (start us, length us, event | category | flops | bytes accessed | tf_op | source)
XLA Modules:
  0.0 50.2 jit_solution(13270502652946854070)
XLA Ops:
  0.6 0.7 %pad_add_fusion.index_ref = s32[30]{0:T(128)S(1)} fusion(s32[10]{0:T(128)} %param.11, s32[20]{0:T(128)} %param.10), kind=kLoop, calls=%fused_computation | loop fusion | flops 30 | bytes 240 | tf_op jit(solution)/shard_map/concatenate | solution.py:489
  1.4 47.7 %shard_map.77 = (bf16[512,640]{1,0:T(8,128)(2,1)S(1)}, f32[3,256,256]{2,1,0:T(8,128)S(1)}) custom-call(s32[30]{0:T(128)S(1)} %pad_add_fusion.index_ref, bf16[512,2560]{1,0:T(8,128)(2,1)} %act_hbm.1, bf16[1728,512]{1,0:T(8,128)(2,1)} %bitcast.3, bf16[1728,2560]{1,0:T(8,128)(2,1)} %bitcast.2, bf16[10,256,256]{2,1,0:T(8,128)(2,1)} %s_hbm.1), custom_call_target="tpu_custom_call" | custom-call | tf_op jit(solution)/shard_map/pallas_call | solution.py:441
  49.1 1.1 %shard_map.78 = (bf16[512,640]{1,0:T(8,128)(2,1)}, f32[3,256,256]{2,1,0:T(8,128)}) custom-call(bf16[512,640]{1,0:T(8,128)(2,1)S(1)} %get-tuple-element.4.a_ref, f32[3,256,256]{2,1,0:T(8,128)S(1)} %get-tuple-element.5.b_ref), custom_call_target="tpu_custom_call" | custom-call | tf_op jit(solution)/shard_map/pallas_call | solution.py:403

commit v5 on v4

--- a/solution.py
+++ b/solution.py
@@ -121,8 +121,6 @@
         tell(i).start()
     for n in range(AHEAD, blocks):
         load_w(n).start()
-    for k in range(tiles):
-        load_act(k).start()
 
     load_cot.wait()
     for i in range(tokens // LANES):
@@ -212,6 +210,8 @@
         eth[b], etl[b] = split(erecv[i])
     rotate(0)
     start_first(0)
+    for k in range(tiles):
+        load_act(k).start()
     for j in range(1, last + 1):
         for n in range(half):
             feature(n, chunks[j])

time: 50.3 us -> 49.7 us (0.988)
  Pallas kernels: 48.8 us -> 48.1 us
    pallas_call x1, Pallas kernels: 47.7 us -> 47 us  [local(): pl.pallas_call(functools.partial(kernel, cfg), out_shape=(jax.ShapeDtypeS...]
where the time goes in v5:
time: 49.7 us; the launch traced here: 49.5 us
  Pallas kernels  48.1 us (97%)
  other arithmetic  0.75 us (2%)
  between operations  0.64 us (1%)
    pallas_call x1, Pallas kernels, local(): pl.pallas_call(functools.partial(kernel, cfg), out_shape=(jax.ShapeDtypeS...  47 us
    pallas_call x1, Pallas kernels, publish(): pl.pallas_call(body, out_shape=(jax.ShapeDtypeStruct(first.shape, first.d...  1.11 us

profile of v5, /device:TPU:0, one launch (start us, length us, event | category | flops | bytes accessed | tf_op | source)
XLA Modules:
  0.0 49.5 jit_solution(9115203945240020298)
XLA Ops:
  0.6 0.7 %pad_add_fusion.index_ref = s32[30]{0:T(128)S(1)} fusion(s32[10]{0:T(128)} %param.11, s32[20]{0:T(128)} %param.10), kind=kLoop, calls=%fused_computation | loop fusion | flops 30 | bytes 240 | tf_op jit(solution)/shard_map/concatenate | solution.py:489
  1.4 47.0 %shard_map.77 = (bf16[512,640]{1,0:T(8,128)(2,1)S(1)}, f32[3,256,256]{2,1,0:T(8,128)S(1)}) custom-call(s32[30]{0:T(128)S(1)} %pad_add_fusion.index_ref, bf16[512,2560]{1,0:T(8,128)(2,1)} %act_hbm.1, bf16[1728,512]{1,0:T(8,128)(2,1)} %bitcast.3, bf16[1728,2560]{1,0:T(8,128)(2,1)} %bitcast.2, bf16[10,256,256]{2,1,0:T(8,128)(2,1)} %s_hbm.1), custom_call_target="tpu_custom_call" | custom-call | tf_op jit(solution)/shard_map/pallas_call | solution.py:441
  48.4 1.1 %shard_map.78 = (bf16[512,640]{1,0:T(8,128)(2,1)}, f32[3,256,256]{2,1,0:T(8,128)}) custom-call(bf16[512,640]{1,0:T(8,128)(2,1)S(1)} %get-tuple-element.4.a_ref, f32[3,256,256]{2,1,0:T(8,128)S(1)} %get-tuple-element.5.b_ref), custom_call_target="tpu_custom_call" | custom-call | tf_op jit(solution)/shard_map/pallas_call | solution.py:403

commit v6 on v5

--- a/solution.py
+++ b/solution.py
@@ -348,6 +348,7 @@
         for o in range(1, n_dp):
             deliver(o).wait_recv()
         share.start()
+        finish(last)
         share.wait_recv()
         scale = 1.0 / math.sqrt(tokens * n_dp)
         for s in range(SLOTS):
@@ -365,7 +366,6 @@
             grad_ref[s, LANES:, LANES:] = lower - lower.T
             grad_ref[s, :LANES, LANES:] = beside
             grad_ref[s, LANES:, :LANES] = -beside.T
-        finish(last)
         for i in range(half):
             swap(i).wait_send()
             cross(i).wait_send()

time: 49.7 us -> 49.9 us (level)
  no operation moved by 1% of the time
where the time goes in v6:
time: 49.9 us; the launch traced here: 49.7 us
  Pallas kernels  48.4 us (97%)
  other arithmetic  0.75 us (2%)
  between operations  0.64 us (1%)
    pallas_call x1, Pallas kernels, local(): pl.pallas_call(functools.partial(kernel, cfg), out_shape=(jax.ShapeDtypeS...  47.2 us
    pallas_call x1, Pallas kernels, publish(): pl.pallas_call(body, out_shape=(jax.ShapeDtypeStruct(first.shape, first.d...  1.11 us

profile of v6, /device:TPU:0, one launch (start us, length us, event | category | flops | bytes accessed | tf_op | source)
XLA Modules:
  0.0 49.7 jit_solution(16104386895696825729)
XLA Ops:
  0.6 0.7 %pad_add_fusion.index_ref = s32[30]{0:T(128)S(1)} fusion(s32[10]{0:T(128)} %param.11, s32[20]{0:T(128)} %param.10), kind=kLoop, calls=%fused_computation | loop fusion | flops 30 | bytes 240 | tf_op jit(solution)/shard_map/concatenate | solution.py:489
  1.4 47.2 %shard_map.77 = (bf16[512,640]{1,0:T(8,128)(2,1)S(1)}, f32[3,256,256]{2,1,0:T(8,128)S(1)}) custom-call(s32[30]{0:T(128)S(1)} %pad_add_fusion.index_ref, bf16[512,2560]{1,0:T(8,128)(2,1)} %act_hbm.1, bf16[1728,512]{1,0:T(8,128)(2,1)} %bitcast.3, bf16[1728,2560]{1,0:T(8,128)(2,1)} %bitcast.2, bf16[10,256,256]{2,1,0:T(8,128)(2,1)} %s_hbm.1), custom_call_target="tpu_custom_call" | custom-call | tf_op jit(solution)/shard_map/pallas_call | solution.py:441
  48.6 1.1 %shard_map.78 = (bf16[512,640]{1,0:T(8,128)(2,1)}, f32[3,256,256]{2,1,0:T(8,128)}) custom-call(bf16[512,640]{1,0:T(8,128)(2,1)S(1)} %get-tuple-element.4.a_ref, f32[3,256,256]{2,1,0:T(8,128)S(1)} %get-tuple-element.5.b_ref), custom_call_target="tpu_custom_call" | custom-call | tf_op jit(solution)/shard_map/pallas_call | solution.py:403
